TPU v7x, 256 devices: a whole 4x4x8 slice. The times are simulated.
256 devices in a mesh: row: 8 (over x, core), col: 16 (over y, z_hi), rep: 2 (over z_lo).
Axes of the slice: x: 4, y: 4, z: 8 (z_hi: 4, z_lo: 2; z = z_hi * 2 + z_lo), core: 2. Of those that a mesh axis runs over, the one named last changes fastest.
Arguments:
- slab_half: float32 [2, 8192, 4096], P('rep', 'row', 'col'), may hold values from -6 to 6
- window_half: float32 [2, 4096, 8192], P('rep', 'row', 'col'), may hold values from -0.125 to 0.125
- slab_cols: int32 [64, 20], replicated, may hold values from 0 to 63, as said below
- window_cols: int32 [64, 20], replicated, may hold values from 0 to 63, as said below
Outputs:
- slab_square: float32 [8192, 8192], P(('row', 'rep'), 'col')
Inputs may be any that keep to these rules, and one draw needn't show every extreme that they name: `slab_cols`: each slab block row i lists 20 distinct block columns, all within 24 blocks of its centre, block column i; it lists the column exactly 24 blocks above the centre where that column exists, else the one exactly 24 blocks below where that exists. `window_cols`: each window block row k lists 20 distinct block columns, all within 24 blocks of column k; it lists column k + 24 where that column exists, else column k - 24 where that exists.
All inputs are finite; a program needn't handle non-finite values.
Results may differ from a plain program's by a relative error of at most 0.0001.
Values sent between devices are 32-bit elements; how exact they have to be, the bound alone decides.
A program may use at most 128 MiB of HBM per device.

v0:
```python
import jax
import jax.numpy as jnp
from jax import lax
from jax.sharding import PartitionSpec as P

BS = 128


def block_mask(columns, width):
    hit = columns[:, :, None] == jnp.arange(width, dtype=jnp.int32)[None, None, :]
    return jnp.any(hit, axis=1)


def expand(mask, size):
    filled = mask.astype(jnp.float32)
    return jnp.repeat(jnp.repeat(filled, size, axis=0), size, axis=1)


def product(left, right):
    return jnp.dot(left, right, precision=lax.Precision.HIGHEST, preferred_element_type=jnp.float32)


def body(slab_half, window_half, slab_cols, window_cols):
    row_index = lax.axis_index("row")
    col_index = lax.axis_index("col")
    rep_index = lax.axis_index("rep")
    window_width = window_cols.shape[0]
    half_blocks = window_width // lax.axis_size("rep")
    slab_blocks = half_blocks // lax.axis_size("col")
    window_blocks = half_blocks // lax.axis_size("row")
    slab_local = slab_half[0]
    window_local = window_half[0]
    row_blocks = slab_local.shape[0] // BS
    col_blocks = window_local.shape[1] // BS
    mask_a = block_mask(slab_cols, window_width)
    mask_b = block_mask(window_cols, window_width)
    half_start = rep_index * half_blocks
    row_start = row_index * row_blocks
    col_start = col_index * col_blocks
    mine_a = lax.dynamic_slice(
        mask_a, (row_start, half_start + col_index * slab_blocks), (row_blocks, slab_blocks)
    )
    mine_b = lax.dynamic_slice(
        mask_b, (half_start + row_index * window_blocks, col_start), (window_blocks, col_blocks)
    )
    slab_kept = slab_local * expand(mine_a, BS)
    window_kept = window_local * expand(mine_b, BS)
    slab_whole = lax.all_gather(slab_kept, "col", axis=1, tiled=True)
    partial_sum = product(slab_whole, lax.all_gather(window_kept, "row", axis=0, tiled=True))
    reduced = lax.psum_scatter(partial_sum, "rep", scatter_dimension=0, tiled=True)
    out_mask = expand(
        lax.dynamic_slice(mask_a, (row_start, col_start), (row_blocks, col_blocks)), BS
    )
    share = reduced.shape[0]
    out_local = lax.dynamic_slice_in_dim(out_mask, rep_index * share, share, 0)
    return reduced * out_local


def solution(mesh):
    in_specs = (P("rep", "row", "col"), P("rep", "row", "col"), P(), P())
    out_specs = P(("row", "rep"), "col")
    return jax.shard_map(body, mesh=mesh, in_specs=in_specs, out_specs=out_specs, check_vma=False)
```

profile of v0, /device:TPU:10, one launch (start us, length us, event | category | flops | bytes accessed | tf_op | source)
XLA Modules:
  0.0 354.5 jit_solution(626893484085413982)
XLA Ops:
  6.5 0.0 copy-start
  6.5 0.0 all-gather.5.cloned.1.call-start
  6.5 1.0 fusion.1
  7.6 0.1 dynamic-slice_convert_fusion.2
  7.7 0.6 broadcast_in_dim.25
  8.3 2.5 bitcast_multiply_fusion
  10.8 0.0 all-gather.5.cloned.1.call-update
  10.8 0.0 all-gather.3.cloned.1.call-start
  10.9 0.9 fusion
  11.8 0.1 dynamic-slice_convert_fusion.1
  11.9 1.2 broadcast_in_dim.23
  13.2 0.0 copy-done
  13.2 1.1 bitcast_multiply_fusion.1
  14.3 0.0 all-gather.3.cloned.1.call-update
  14.3 0.0 reduce-scatter.2.cloned.1.call-start
  14.4 50.8 %all-gather.5.cloned.1.call-done = f32[4096,512]{1,0:T(8,128)} async-done(((f32[512,512]{1,0:T(8,128)}), f32[4096,512]{1,0:T(8,128)}) %all-gather.5.cloned.1.call-update) | async-done | bytes 8388624 | tf_op jit(solution)/shard_map/all_gather | solution.py:49
  65.2 212.3 %all-gather.3.cloned.1.call-done = f32[1024,4096]{1,0:T(8,128)} async-done(((f32[1024,256]{1,0:T(8,128)}), f32[1024,4096]{1,0:T(8,128)}) %all-gather.3.cloned.1.call-update) | async-done | bytes 16777232 | tf_op jit(solution)/shard_map/all_gather | solution.py:48
  277.5 31.0 %fusion.2 = f32[1024,512]{1,0:T(8,128)} fusion(f32[1024,4096]{1,0:T(8,128)} %all-gather.3.cloned.1.call-done, f32[4096,512]{1,0:T(8,128)} %all-gather.5.cloned.1.call-done), kind=kOutput, calls=%fused_computation.11 | convolution fusion | flops 25769803776 | bytes 27262976 | tf_op jit(solution)/shard_map/dot_general | solution.py:20
  308.5 0.0 reduce-scatter.2.cloned.1.call-update
  308.6 0.1 dynamic-slice_convert_fusion
  308.7 1.2 broadcast_in_dim.27
  309.9 0.2 copy.13
  310.1 35.4 %reduce-scatter.2.cloned.1.call-done = f32[512,512]{1,0:T(8,128)} async-done(((f32[1024,512]{1,0:T(8,128)}), f32[512,512]{1,0:T(8,128)}) %reduce-scatter.2.cloned.1.call-update) | async-done | bytes 1048592 | tf_op jit(solution)/shard_map/reduce_scatter | solution.py:50
  345.5 2.4 dynamic-slice_multiply_fusion
  (3 shorter events, 0.1 us)
Async XLA Ops:
  6.5 6.6 %copy-start = (f32[1,1024,256]{2,1,0:T(8,128)S(1)}, f32[1,1024,256]{2,1,0:T(8,128)}, u32[]{:S(2)}) copy-start(f32[1,1024,256]{2,1,0:T(8,128)} %param.4) | copy-start | bytes 3145732
  6.5 58.7 %all-gather.5.cloned.1.call-start = ((), (), s32[]{:S(2)}) async-start(), calls=%async_computation.2 | async-start | bytes 9437184 | tf_op jit(solution)/shard_map/all_gather | solution.py:49
  10.8 266.7 %all-gather.3.cloned.1.call-start = ((), (), s32[]{:S(2)}) async-start(), calls=%async_computation.1 | async-start | bytes 17825792 | tf_op jit(solution)/shard_map/all_gather | solution.py:48
  14.3 331.2 %reduce-scatter.2.cloned.1.call-start = ((), (), s32[]{:S(2)}) async-start(), calls=%async_computation.3 | async-start | bytes 3145728 | tf_op jit(solution)/shard_map/reduce_scatter | solution.py:50
Sparse Core Ops, SparseCore 0:
  10.9 54.2 all-gather.4
  67.6 209.8 all-gather.2
  308.7 36.7 reduce-scatter.1
where the time goes:
time: 355 us; the launch traced here: 354 us
  waiting for transfers between devices  299 us (84%)
  matrix products  31 us (9%)
  between operations  13.2 us (4%)
  other arithmetic  8.21 us (2%)
    all_gather x1, waiting for transfers between devices, body(): slab_whole = lax.all_gather(slab_kept, 'col', axis=1, tiled=True)  212 us
    all_gather x1, waiting for transfers between devices, body(): lax.all_gather(window_kept, 'row', axis=0, tiled=True)  50.8 us
    reduce_scatter x1, waiting for transfers between devices, body(): lax.psum_scatter(partial_sum, 'rep', scatter_dimension=0, tiled=True)  35.4 us
    dot_general x1, matrix products, product(): jnp.dot(left, right, precision=lax.Precision.HIGHEST, preferred_element_t...  31 us
  transfers between devices with their start and end apart: 3, of which 3 were waited for; matrix products, arithmetic and copies ran while one was open for 1% of the time, Pallas kernels for 0%

commit v1 on v0

v1 whole, which is shorter than its diff:
```python
import jax
import jax.numpy as jnp
from jax import lax
from jax.experimental import pallas as pl
from jax.experimental.pallas import tpu as pltpu
from jax.sharding import PartitionSpec as P

BS = 128
BAND = 24
KL = 20
MESH = pl.DeviceIdType.MESH
G = 4
W = BAND // G
NG = 16
T = G * BS
NX, NY, NZ = 4, 4, 8
NEAR = (0, -1, 1, -2, 2, -3, 3, 4)


def close(a, b):
    return (a - b <= W) & (b - a <= W)


def gather_kernel(slab, window, a_out, b_out, bounce_a, bounce_b, local_sem, za_recv, b_recv, share_recv,
                  z_send, zr_send, y_send, yr_send, x_send, xr_send, c_send, s_send):
    row, col, rep = lax.axis_index("row"), lax.axis_index("col"), lax.axis_index("rep")
    x, core = row // 2, row % 2
    y, zh = col // 4, col % 4
    z = zh * 2 + rep
    mine = 2 * row + rep
    other = 2 * row + 1 - rep

    def at_z(off):
        t = (z + off + NZ) % NZ
        return {"row": row, "col": y * 4 + t // 2, "rep": t % 2}

    def at_y(off):
        return {"row": row, "col": ((y + off + NY) % NY) * 4 + zh, "rep": rep}

    def at_x(off):
        return {"row": ((x + off + NX) % NX) * 2 + core, "col": col, "rep": rep}

    partner = {"row": x * 2 + 1 - core, "col": col, "rep": rep}
    across = {"row": row, "col": col, "rep": 1 - rep}

    barrier = pltpu.get_barrier_semaphore()
    friends = [at_z(1), at_z(-1), at_z(2), at_z(-2), at_y(1), at_y(-1), at_x(1), at_x(-1), partner]
    for f in friends:
        pl.semaphore_signal(barrier, inc=1, device_id=f, device_id_type=MESH)
    pl.semaphore_wait(barrier, len(friends))

    later = []

    def begin(cond, copy):
        @pl.when(cond)
        def _():
            copy.start()

        @later.append
        def _():
            @pl.when(cond)
            def _():
                copy.wait_send()

    def piece_of(off, ys):
        s = (z + off + NZ) % NZ
        q = (s % 2) * 16 + ys * 4 + s // 2
        return q, q // 2

    H = T // 2

    def a_half(q, h):
        return a_out.at[q, pl.ds(h * H, H)]

    def a_copy(src, q, h, send, dest):
        return pltpu.make_async_remote_copy(
            src_ref=src, dst_ref=a_half(q, h), send_sem=send, recv_sem=za_recv.at[q, h],
            device_id=dest, device_id_type=MESH)

    def a_wait(q, h, cond):
        @pl.when(cond)
        def _():
            pltpu.make_async_remote_copy(
                src_ref=a_half(q, h), dst_ref=a_half(q, h), send_sem=za_recv.at[q, h],
                recv_sem=za_recv.at[q, h], device_id=at_z(1), device_id_type=MESH).wait_recv()

    def b_half(k, h):
        return b_out.at[k, pl.ds(h * H, H)]

    def b_copy(src, k, h, send, recv, dest):
        return pltpu.make_async_remote_copy(
            src_ref=src, dst_ref=b_half(k, h), send_sem=send, recv_sem=recv.at[k, h],
            device_id=dest, device_id_type=MESH)

    def b_wait(k, h, cond, recv):
        @pl.when(cond)
        def _():
            pltpu.make_async_remote_copy(
                src_ref=b_half(k, h), dst_ref=b_half(k, h), send_sem=recv.at[k, h],
                recv_sem=recv.at[k, h], device_id=at_z(1), device_id_type=MESH).wait_recv()

    q0, k0 = piece_of(0, y)
    own_in = close(mine, k0)
    opp_in = close(other, k0)

    def own(parity, h):
        return slab.at[0, pl.ds(parity * T + h * H, H)]

    for h in range(2):
        begin(opp_in, a_copy(own(1 - rep, h), q0, h, z_send.at[0, h], at_z(1)))
        begin(opp_in, a_copy(own(1 - rep, h), q0, h, z_send.at[1, h], at_z(-1)))
    for h in range(2):
        begin(own_in, a_copy(own(rep, h), q0, h, z_send.at[2, h], at_z(2)))
        begin(own_in, a_copy(own(rep, 1 - h), q0, 1 - h, z_send.at[3, 1 - h], at_z(-2)))

    kb = rep * 8 + row
    kc = (1 - rep) * 8 + row
    kb_in, kc_in = close(kb, col), close(kc, col)

    def b_first(k, cond, src, n):
        for h in range(2):
            begin(cond, b_copy(src(h), k, h, x_send.at[n, 0, h], b_recv, at_x(1 if h == 0 else -1)))
        for h in range(2):
            begin(cond, b_copy(src(h), k, h, x_send.at[n, 1, h], b_recv, at_x(-1 if h == 0 else 1)))
        for h in range(2):
            begin(cond, b_copy(src(h), k, h, s_send.at[n, h], share_recv, partner))

    def own_b(h):
        return window.at[0, pl.ds(h * H, H)]

    for h in range(2):
        begin(kb_in, b_copy(own_b(h), kb, h, c_send.at[h], b_recv, across))
    b_first(kb, kb_in, own_b, 0)

    in_a = pltpu.make_async_copy(slab.at[0, pl.ds(rep * T, T)], bounce_a, local_sem.at[0])
    in_b = pltpu.make_async_copy(window.at[0], bounce_b, local_sem.at[1])
    in_a.start()
    in_b.start()

    def wants(k, yd):
        c = ((yd + NY) % NY) * 4 + zh
        return close(mine, k) & close(c, k) & close(mine, c)

    def y_first(n):
        q, k = piece_of(NEAR[n], y)
        up, down, far = wants(k, y + 1), wants(k, y - 1), wants(k, y + 2)
        for h in range(2):
            src = own(rep, h) if n == 0 else a_half(q, h)
            begin(up | far if h == 0 else up, a_copy(src, q, h, y_send.at[n, 0, h], at_y(1)))
        for h in (1, 0):
            src = own(rep, h) if n == 0 else a_half(q, h)
            begin(down | far if h == 1 else down, a_copy(src, q, h, y_send.at[n, 1, h], at_y(-1)))

    def y_relay(n):
        here_next = None
        q, k = piece_of(NEAR[n], (y + NY - 1) % NY)
        need, onward = wants(k, y), wants(k, y + 1)
        a_wait(q, 0, need | onward)
        begin(onward, a_copy(a_half(q, 0), q, 0, yr_send.at[n, 0], at_y(1)))
        q2, k2 = piece_of(NEAR[n], (y + 1) % NY)
        need2, onward2 = wants(k2, y), wants(k2, y - 1)
        a_wait(q2, 1, need2 | onward2)
        begin(onward2, a_copy(a_half(q2, 1), q2, 1, yr_send.at[n, 1], at_y(-1)))

    def y_rest(n):
        q, k = piece_of(NEAR[n], (y + NY - 1) % NY)
        a_wait(q, 1, wants(k, y))
        q, k = piece_of(NEAR[n], (y + 1) % NY)
        a_wait(q, 0, wants(k, y))
        q, k = piece_of(NEAR[n], (y + 2) % NY)
        for h in range(2):
            a_wait(q, h, wants(k, y))

    y_first(0)

    for n, d in ((1, -1), (2, 1)):
        q, k = piece_of(d, y)
        c = close(mine, k)
        for h in range(2):
            a_wait(q, h, c)
            begin(c, a_copy(a_half(q, h), q, h, zr_send.at[n - 1, h], at_z(-2 * d)))
        y_first(n)
    y_relay(0)

    for n, d, h in ((3, -2, 0), (4, 2, 1)):
        q, k = piece_of(d, y)
        c = close(mine, k)
        a_wait(q, h, c)
        begin(c, a_copy(a_half(q, h), q, h, zr_send.at[2, h], at_z(-d)))
        a_wait(q, 1 - h, c)
        y_first(n)
    y_relay(1)

    for h in range(2):
        b_wait(kc, h, kc_in, b_recv)
    b_first(kc, kc_in, lambda h: b_half(kc, h), 1)

    def b_from(n, off):
        p = rep if n == 0 else 1 - rep
        k = p * 8 + ((x + off + NX) % NX) * 2 + core
        return k, close(k, col)

    def b_relay(n):
        for off, h in ((-1, 0), (1, 1)):
            k, cond = b_from(n, off)
            b_wait(k, h, cond, b_recv)
            begin(cond, b_copy(b_half(k, h), k, h, xr_send.at[n, h], b_recv, at_x(-off)))
            begin(cond, b_copy(b_half(k, h), k, h, s_send.at[2 + n * 3 + (off + 1) // 2, h], share_recv, partner))

    def b_rest(n):
        for off, h in ((-1, 1), (1, 0)):
            k, cond = b_from(n, off)
            b_wait(k, h, cond, b_recv)
            begin(cond, b_copy(b_half(k, h), k, h, s_send.at[2 + n * 3 + (off + 1) // 2, h], share_recv, partner))
        k, cond = b_from(n, 2)
        for h in range(2):
            b_wait(k, h, cond, b_recv)
            begin(cond, b_copy(b_half(k, h), k, h, s_send.at[2 + n * 3 + 2, h], share_recv, partner))

    b_relay(0)
    y_relay(2)

    for n, d in ((5, -3), (6, 3), (7, 4)):
        q, k = piece_of(d, y)
        for h in range(2):
            a_wait(q, h, close(mine, k))
        y_first(n)
        y_relay(n - 2)
    b_relay(1)
    b_rest(0)
    y_relay(6)
    y_relay(7)
    b_rest(1)

    in_a.wait()
    in_b.wait()
    put_a = pltpu.make_async_copy(bounce_a, a_out.at[q0], local_sem.at[2])
    put_b = pltpu.make_async_copy(bounce_b, b_out.at[kb], local_sem.at[3])
    put_a.start()
    put_b.start()

    for n in range(8):
        y_rest(n)
    for m in range(8):
        k = m * 2 + 1 - core
        for h in range(2):
            b_wait(k, h, close(k, col), share_recv)
    put_a.wait()
    put_b.wait()
    for end in later:
        end()


def gather(slab, window):
    dma = pltpu.SemaphoreType.DMA
    hbm = pl.BlockSpec(memory_space=pl.ANY)
    return pl.pallas_call(
        gather_kernel,
        out_shape=(jax.ShapeDtypeStruct((2 * NG, T, T // 2), jnp.float32),
                   jax.ShapeDtypeStruct((NG, T, T), jnp.float32)),
        in_specs=[hbm, hbm],
        out_specs=(hbm, hbm),
        scratch_shapes=[
            pltpu.VMEM((T, T // 2), jnp.float32), pltpu.VMEM((T, T), jnp.float32),
            dma((4,)), dma((2 * NG, 2)), dma((NG, 2)), dma((NG, 2)),
            dma((4, 2)), dma((3, 2)), dma((8, 2, 2)), dma((8, 2)),
            dma((2, 2, 2)), dma((2, 2)), dma((2,)), dma((8, 2)),
        ],
        compiler_params=pltpu.CompilerParams(collective_id=0, has_side_effects=True),
        name="gather",
    )(slab, window)


def split(v):
    high = v.astype(jnp.bfloat16)
    return high, (v - high.astype(jnp.float32)).astype(jnp.bfloat16)


def product_kernel(span, slab_cols, window_cols, a_ref, b_ref, out_ref):
    s = pl.program_id(0)
    lo, count, rows, cols = span[0], span[1], span[2], span[3]
    lane = lax.broadcasted_iota(jnp.int32, (1, T), 1) // BS

    def listed(table, at, first):
        hit = jnp.zeros((1, T), jnp.float32)
        for t in range(KL):
            hit = jnp.where(lane == table[at, t] - first, 1.0, hit)
        return hit

    @pl.when(s == 0)
    def _():
        out_ref[...] = jnp.zeros_like(out_ref)

    @pl.when(s < count)
    def _():
        k = lo + s
        left, right = [], []
        for i in range(G):
            keep = listed(slab_cols, rows * G + i, k * G)
            part = jnp.concatenate([a_ref[0, 0, i * BS:(i + 1) * BS], a_ref[0, 1, i * BS:(i + 1) * BS]], axis=1)
            left.append(part * keep)
            keep = listed(window_cols, k * G + i, cols * G)
            right.append(b_ref[0, i * BS:(i + 1) * BS] * keep)
        lh, ll = split(jnp.concatenate(left, axis=0))
        rh, rl = split(jnp.concatenate(right, axis=0))
        dot = lambda u, v: jnp.dot(u, v, preferred_element_type=jnp.float32)
        out_ref[...] += dot(lh, rh) + (dot(lh, rl) + dot(ll, rh))

    @pl.when(s == pl.num_programs(0) - 1)
    def _():
        for i in range(G):
            part = slice(i * BS, (i + 1) * BS)
            out_ref[part, :] = out_ref[part, :] * listed(slab_cols, rows * G + i, cols * G)


def multiply(span, slab_cols, window_cols, a, b):
    at = lambda s, span, *_: (span[0] + jnp.minimum(s, jnp.maximum(span[1] - 1, 0)), 0, 0)
    at4 = lambda s, span, *_: (span[0] + jnp.minimum(s, jnp.maximum(span[1] - 1, 0)), 0, 0, 0)
    return pl.pallas_call(
        product_kernel,
        grid_spec=pltpu.PrefetchScalarGridSpec(
            num_scalar_prefetch=3, grid=(2 * W + 1,),
            in_specs=[pl.BlockSpec((1, 2, T, T // 2), at4), pl.BlockSpec((1, T, T), at)],
            out_specs=pl.BlockSpec((T, T), lambda s, *_: (0, 0))),
        out_shape=jax.ShapeDtypeStruct((T, T), jnp.float32),
        compiler_params=pltpu.CompilerParams(dimension_semantics=("arbitrary",)),
        name="multiply",
    )(span, slab_cols, window_cols, a.reshape(NG, 2, T, T // 2), b)


def body(slab_half, window_half, slab_cols, window_cols):
    mine = 2 * lax.axis_index("row") + lax.axis_index("rep")
    col = lax.axis_index("col")
    a, b = gather(slab_half, window_half)
    lo = jnp.maximum(jnp.maximum(mine, col) - W, 0)
    hi = jnp.minimum(jnp.minimum(mine, col) + W, NG - 1)
    count = jnp.where(close(mine, col), jnp.maximum(hi - lo + 1, 0), 0)
    span = jnp.stack([jnp.minimum(lo, NG - 1), count, mine, col]).astype(jnp.int32)
    return multiply(span, slab_cols, window_cols, a, b)


def solution(mesh):
    in_specs = (P("rep", "row", "col"), P("rep", "row", "col"), P(), P())
    out_specs = P(("row", "rep"), "col")
    return jax.shard_map(body, mesh=mesh, in_specs=in_specs, out_specs=out_specs, check_vma=False)
```

time: 355 us -> 171 us (0.48)
  waiting for transfers between devices: 299 us -> 0 us
  Pallas kernels: 0 us -> 167 us
  matrix products: 31 us -> 0 us
  between operations: 13.2 us -> 0.01 us
  other arithmetic: 8.21 us -> 0.61 us
    all_gather x2 -> x0, waiting for transfers between devices: 263 us -> none  [the longest x1 212 us: body(): slab_whole = lax.all_gather(slab_kept, 'col', axis=1, tiled=True)]
    pallas_call x0 -> x2, Pallas kernels: none -> 167 us  [the longest x1 148 us: gather(): pl.pallas_call(gather_kernel, out_shape=(jax.ShapeDtypeStruct((2 * NG, T,...]
    reduce_scatter x1 -> x0, waiting for transfers between devices: 35.4 us -> none  [body(): lax.psum_scatter(partial_sum, 'rep', scatter_dimension=0, tiled=True)]
    dot_general x1 -> x0, matrix products: 31 us -> none  [product(): jnp.dot(left, right, precision=lax.Precision.HIGHEST, preferred_element_t...]
    mul x3 -> x0, other arithmetic: 5.99 us -> none  [the longest x1 2.49 us: body(): window_kept = window_local * expand(mine_b, BS)]
  transfers between devices with their start and end apart: 3 -> 0, of which waited for: 3 -> 0; matrix products, arithmetic and copies ran while one was open for 1% -> 0% of each run, Pallas kernels for 0% -> 0%
where the time goes in v1:
time: 171 us
  Pallas kernels  167 us (98%)
  local copies, waits for them, and re-layouts  2.79 us (2%)
    pallas_call x1, Pallas kernels, gather(): pl.pallas_call(gather_kernel, out_shape=(jax.ShapeDtypeStruct((2 * NG, T,...  148 us
    pallas_call x1, Pallas kernels, multiply(): pl.pallas_call(product_kernel, grid_spec=pltpu.PrefetchScalarGridSpec(num...  19.6 us

profile of v1, /device:TPU:10, one launch (start us, length us, event | category | flops | bytes accessed | tf_op | source)
XLA Modules:
  0.0 170.7 jit_solution(14705635074585313309)
XLA Ops:
  0.0 0.6 pad_add_fusion.span
  0.6 1.4 copy.5.slab_cols
  2.0 1.4 copy.6.window_cols
  3.4 147.8 %gather.1 = (f32[32,512,256]{2,1,0:T(8,128)}, f32[16,512,512]{2,1,0:T(8,128)}) custom-call(f32[1,1024,256]{2,1,0:T(8,128)} %slab.1, f32[1,512,512]{2,1,0:T(8,128)} %window.1), custom_call_target="tpu_custom_call" | custom-call | tf_op jit(solution)/shard_map/gather/pallas_call | solution.py:257
  151.2 19.6 %multiply.1 = f32[512,512]{1,0:T(8,128)} custom-call(s32[4]{0:T(128)} %pad_add_fusion.span, s32[64,20]{1,0:T(8,128)} %copy.5.slab_cols, s32[64,20]{1,0:T(8,128)} %copy.6.window_cols, f32[16,2,512,256]{3,2,1,0:T(8,128)} %bitcast.5, f32[16,512,512]{2,1,0:T(8,128)} %get-tuple-element.8.b_ref), custom_call_target="tpu_custom_call" | custom-call | tf_op jit(solution)/shard_map/multiply/pallas_call | solution.py:319

commit v2 on v0

v2 whole, which is shorter than its diff:
```python
import jax
import jax.numpy as jnp
from jax import lax
from jax.experimental import pallas as pl
from jax.experimental.pallas import tpu as pltpu
from jax.sharding import PartitionSpec as P

BS = 128
BAND = 24
KL = 20
MESH = pl.DeviceIdType.MESH
G = 4
W = BAND // G
NG = 16
T = G * BS
NX, NY, NZ, NH = 4, 4, 8, 4
ST = T // NG
HK = KL // 2
HT = T // 2


def close(a, b):
    return (a - b <= W) & (b - a <= W)


def gather_kernel(slab, window, slab_cols, g_out, b_out, strips, packed, bounce, local_sem, e_recv, g_recv, b_recv,
                  share_recv, e_send, z_send, zr_send, y_send, yr_send, x_send, xr_send, c_send, s_send):
    row, col, rep = lax.axis_index("row"), lax.axis_index("col"), lax.axis_index("rep")
    x, core = row // 2, row % 2
    y, zh = col // NH, col % NH
    z = zh * 2 + rep
    mine = 2 * row + rep
    other = 2 * row + 1 - rep

    def at_plane(oy, oz):
        t = (z + oz) % NZ
        return {"row": row, "col": ((y + oy) % NY) * NH + t // 2, "rep": t % 2}

    def at_h(off):
        return {"row": row, "col": y * NH + (zh + off + NH) % NH, "rep": rep}

    def at_y(off):
        return {"row": row, "col": ((y + off + NY) % NY) * NH + zh, "rep": rep}

    def at_x(off):
        return {"row": ((x + off + NX) % NX) * 2 + core, "col": col, "rep": rep}

    partner = {"row": x * 2 + 1 - core, "col": col, "rep": rep}
    across = {"row": row, "col": col, "rep": 1 - rep}
    plane = [(oy, oz) for oz in (4, 3, 5, 2, 6, 1, 7, 0) for oy in (2, 1, 3, 0) if (oy, oz) != (0, 0)]

    barrier = pltpu.get_barrier_semaphore()
    friends = [at_plane(oy, oz) for oy, oz in plane] + [at_x(1), at_x(-1), partner]
    for f in friends:
        pl.semaphore_signal(barrier, inc=1, device_id=f, device_id_type=MESH)
    pl.semaphore_wait(barrier, len(friends))

    later = []

    def begin(cond, copy):
        @pl.when(cond)
        def _():
            copy.start()

        @later.append
        def _():
            @pl.when(cond)
            def _():
                copy.wait_send()

    def send(src, dst, sem, recv, dest):
        return pltpu.make_async_remote_copy(
            src_ref=src, dst_ref=dst, send_sem=sem, recv_sem=recv, device_id=dest, device_id_type=MESH)

    def landed(cond, dst, recv):
        @pl.when(cond)
        def _():
            send(dst, dst, recv, recv, partner).wait_recv()

    q0 = rep * NG + col
    k0 = q0 // 2
    own_in, opp_in = close(mine, k0), close(other, k0)

    def rows_for(p, c):
        return slab.at[0, pl.ds(p * T + c * ST, ST)]

    for n, (oy, oz) in enumerate(plane):
        d = at_plane(oy, oz)
        begin(own_in if oz % 2 == 0 else opp_in,
              send(rows_for(d["rep"], d["col"]), strips.at[q0], e_send.at[n], e_recv.at[q0], d))
    keep_strip = pltpu.make_async_copy(rows_for(rep, col), strips.at[q0], local_sem.at[0])
    keep_strip.start()

    def b_half(k, h):
        return b_out.at[k, pl.ds(h * HT, HT)]

    def own_b(h):
        return window.at[0, pl.ds(h * HT, HT)]

    def wants_b(k, xd):
        first = 4 * ((xd + NX) % NX) + rep
        second = first + 2
        return close(k, col) & ((close(first, col) & close(first, k)) | (close(second, col) & close(second, k)))

    twin = 2 * (x * 2 + 1 - core) + rep

    def b_share(k, h, src, n):
        cond = close(k, col) & close(twin, col) & close(twin, k)
        begin(cond, send(src, b_half(k, h), s_send.at[n, h], share_recv.at[k, h], partner))

    def b_first(k, src, n):
        up, down, far = wants_b(k, x + 1), wants_b(k, x - 1), wants_b(k, x + 2)
        for lead in (0, 1):
            h = lead
            begin(up | far if lead == 0 else up,
                  send(src(h), b_half(k, h), x_send.at[n, 0, h], b_recv.at[k, h], at_x(1)))
            h = 1 - lead
            begin(down | far if lead == 0 else down,
                  send(src(h), b_half(k, h), x_send.at[n, 1, h], b_recv.at[k, h], at_x(-1)))
        for h in range(2):
            b_share(k, h, src(h), n)

    kb = rep * 8 + row
    kc = (1 - rep) * 8 + row
    kb_in, kc_in = close(kb, col), close(kc, col)
    for h in range(2):
        begin(kb_in, send(own_b(h), b_half(kb, h), c_send.at[h], b_recv.at[kb, h], across))
    b_first(kb, own_b, 0)
    take_b = pltpu.make_async_copy(window.at[0], bounce, local_sem.at[1])
    take_b.start()

    def b_from(n, off):
        p = rep if n == 0 else 1 - rep
        return p * 8 + ((x + off + NX) % NX) * 2 + core

    def b_relay(n):
        for off, h in ((-1, 0), (1, 1)):
            k = b_from(n, off)
            onward = wants_b(k, x - off)
            landed(wants_b(k, x) | onward, b_half(k, h), b_recv.at[k, h])
            begin(onward, send(b_half(k, h), b_half(k, h), xr_send.at[n, h], b_recv.at[k, h], at_x(-off)))
            b_share(k, h, b_half(k, h), 2 + n * 3 + (off + 1) // 2)

    def b_rest(n):
        for off, h in ((-1, 1), (1, 0)):
            k = b_from(n, off)
            landed(wants_b(k, x), b_half(k, h), b_recv.at[k, h])
            b_share(k, h, b_half(k, h), 2 + n * 3 + (off + 1) // 2)
        k = b_from(n, 2)
        for h in range(2):
            landed(wants_b(k, x), b_half(k, h), b_recv.at[k, h])
            b_share(k, h, b_half(k, h), 2 + n * 3 + 2)

    take_b.wait()
    put_b = pltpu.make_async_copy(bounce, b_out.at[kb], local_sem.at[2])
    put_b.start()
    b_relay(0)

    keep_strip.wait()
    for oz in range(NZ):
        for oy in range(NY):
            if (oy, oz) == (0, 0):
                continue
            t = (z + oz) % NZ
            q = (t % 2) * NG + ((y + oy) % NY) * NH + t // 2
            landed(close(mine, q // 2), strips.at[q], e_recv.at[q])
    for t in range(KL):
        k = slab_cols[mine * G + y, t]
        both = strips[k // 2]
        packed[t] = jnp.where(k % 2 == 0, both[:, :BS], both[:, BS:])

    def place(i, s, h):
        return g_out.at[i, pl.ds(h * HK, HK), pl.ds(s * ST, ST)]

    def own_g(h):
        return packed.at[pl.ds(h * HK, HK)]

    def g_send(src, i, s, h, sem, dest):
        return send(src, place(i, s, h), sem, g_recv.at[i, s, h], dest)

    always = rep >= 0

    def wants_g(yd):
        return close(mine, ((yd + NY) % NY) * NH + zh)

    here, up, down, far = wants_g(y), wants_g(y + 1), wants_g(y - 1), wants_g(y + 2)

    for lead in range(2):
        begin(always, g_send(own_g(lead), y, zh, lead, z_send.at[0, lead], at_h(1)))
        begin(always, g_send(own_g(1 - lead), y, zh, 1 - lead, z_send.at[1, 1 - lead], at_h(-1)))

    def y_first(n, off):
        s = (zh + off + NH) % NH
        for lead in range(2):
            h = lead
            begin(up | far if lead == 0 else up,
                  g_send(own_g(h) if n == 0 else place(y, s, h), y, s, h, y_send.at[n, 0, h], at_y(1)))
            h = 1 - lead
            begin(down | far if lead == 0 else down,
                  g_send(own_g(h) if n == 0 else place(y, s, h), y, s, h, y_send.at[n, 1, h], at_y(-1)))

    def y_relay(n, off):
        s = (zh + off + NH) % NH
        for d, h in ((-1, 0), (1, 1)):
            i = (y + d + NY) % NY
            onward = wants_g(y - d)
            landed(here | onward, place(i, s, h), g_recv.at[i, s, h])
            begin(onward, g_send(place(i, s, h), i, s, h, yr_send.at[n, h], at_y(-d)))

    def y_rest(n, off):
        s = (zh + off + NH) % NH
        for d, h in ((-1, 1), (1, 0), (2, 0), (2, 1)):
            i = (y + d + NY) % NY
            landed(here, place(i, s, h), g_recv.at[i, s, h])

    y_first(0, 0)
    put_g = pltpu.make_async_copy(packed, g_out.at[y, :, pl.ds(zh * ST, ST)], local_sem.at[3])
    put_g.start()

    for h in range(2):
        landed(kc_in, b_half(kc, h), b_recv.at[kc, h])
    b_first(kc, lambda h: b_half(kc, h), 1)

    for n, off, h in ((1, -1, 0), (2, 1, 1)):
        s = (zh + off + NH) % NH
        landed(always, place(y, s, h), g_recv.at[y, s, h])
        begin(always, g_send(place(y, s, h), y, s, h, zr_send.at[h], at_h(-off)))
    b_rest(0)
    for n, off, h in ((1, -1, 1), (2, 1, 0)):
        s = (zh + off + NH) % NH
        landed(always, place(y, s, h), g_recv.at[y, s, h])
        y_first(n, off)
    y_relay(0, 0)
    s = (zh + 2) % NH
    for h in range(2):
        landed(always, place(y, s, h), g_recv.at[y, s, h])
    y_first(3, 2)
    y_relay(1, -1)
    b_relay(1)
    y_relay(2, 1)
    y_relay(3, 2)
    b_rest(1)

    for n, off in enumerate((0, -1, 1, 2)):
        y_rest(n, off)
    for m in range(8):
        k = m * 2 + 1 - core
        for h in range(2):
            landed(close(k, col) & close(mine, col) & close(mine, k), b_half(k, h), share_recv.at[k, h])
    put_g.wait()
    put_b.wait()
    for end in later:
        end()


def gather(slab, window, slab_cols):
    dma = pltpu.SemaphoreType.DMA
    hbm = pl.BlockSpec(memory_space=pl.ANY)
    return pl.pallas_call(
        gather_kernel,
        out_shape=(jax.ShapeDtypeStruct((G, KL, BS, BS), jnp.float32),
                   jax.ShapeDtypeStruct((NG, T, T), jnp.float32)),
        in_specs=[hbm, hbm, pl.BlockSpec(memory_space=pltpu.SMEM)],
        out_specs=(hbm, hbm),
        scratch_shapes=[
            pltpu.VMEM((2 * NG, ST, 2 * BS), jnp.float32), pltpu.VMEM((KL, ST, BS), jnp.float32),
            pltpu.VMEM((T, T), jnp.float32),
            dma((4,)), dma((2 * NG,)), dma((NY, NH, 2)), dma((NG, 2)), dma((NG, 2)),
            dma((31,)), dma((2, 2)), dma((2,)), dma((4, 2, 2)), dma((4, 2)),
            dma((2, 2, 2)), dma((2, 2)), dma((2,)), dma((8, 2)),
        ],
        compiler_params=pltpu.CompilerParams(collective_id=0, has_side_effects=True),
        name="gather",
    )(slab, window, slab_cols)


def split(v):
    high = v.astype(jnp.bfloat16)
    return high, (v - high.astype(jnp.float32)).astype(jnp.bfloat16)


STEPS = 2 * W + 1


def product_kernel(span, slab_cols, window_cols, g_ref, b_ref, out_ref, b_high, b_low):
    s = pl.program_id(0)
    lo, count, rows, cols = span[0], span[1], span[2], span[3]
    lane = lax.broadcasted_iota(jnp.int32, (1, T), 1) // BS

    def listed(table, at, first):
        hit = jnp.zeros((1, T), jnp.float32)
        for t in range(KL):
            hit = jnp.where(lane == table[at, t] - first, 1.0, hit)
        return hit

    @pl.when(s < count)
    def _():
        for i in range(G):
            keep = listed(window_cols, (lo + s) * G + i, cols * G)
            high, low = split(b_ref[0, i * BS:(i + 1) * BS] * keep)
            b_high[s * G + i] = high
            b_low[s * G + i] = low

    @pl.when((s >= STEPS) & (count == 0))
    def _():
        out_ref[...] = jnp.zeros_like(out_ref)

    @pl.when((s >= STEPS) & (count > 0))
    def _():
        at = rows * G + s - STEPS
        total = jnp.zeros((BS, T), jnp.float32)
        for t in range(0, KL, 2):
            left, high, low = [], [], []
            for u in (t, t + 1):
                k = slab_cols[at, u] - lo * G
                valid = (k >= 0) & (k < count * G)
                k = jnp.where(valid, k, 0)
                left.append(g_ref[0, u] * jnp.where(valid, 1.0, 0.0))
                high.append(b_high[k])
                low.append(b_low[k])
            lh, ll = split(jnp.concatenate(left, axis=1))
            rh, rl = jnp.concatenate(high, axis=0), jnp.concatenate(low, axis=0)
            two = jnp.dot(jnp.concatenate([lh, ll], axis=0), rh, preferred_element_type=jnp.float32)
            total = total + (two[:BS] + (two[BS:] + jnp.dot(lh, rl, preferred_element_type=jnp.float32)))
        out_ref[...] = total * listed(slab_cols, at, cols * G)


def multiply(span, slab_cols, window_cols, g, b):
    at_b = lambda s, span, *_: (span[0] + jnp.minimum(s, jnp.maximum(span[1] - 1, 0)), 0, 0)
    at_g = lambda s, *_: (jnp.maximum(s - STEPS, 0), 0, 0, 0)
    return pl.pallas_call(
        product_kernel,
        grid_spec=pltpu.PrefetchScalarGridSpec(
            num_scalar_prefetch=3, grid=(STEPS + G,),
            in_specs=[pl.BlockSpec((1, KL, BS, BS), at_g), pl.BlockSpec((1, T, T), at_b)],
            out_specs=pl.BlockSpec((BS, T), lambda s, *_: (jnp.maximum(s - STEPS, 0), 0)),
            scratch_shapes=[pltpu.VMEM((STEPS * G, BS, T), jnp.bfloat16)] * 2),
        out_shape=jax.ShapeDtypeStruct((T, T), jnp.float32),
        compiler_params=pltpu.CompilerParams(dimension_semantics=("arbitrary",)),
        name="multiply",
    )(span, slab_cols, window_cols, g, b)


def body(slab_half, window_half, slab_cols, window_cols):
    mine = 2 * lax.axis_index("row") + lax.axis_index("rep")
    col = lax.axis_index("col")
    g, b = gather(slab_half, window_half, slab_cols)
    lo = jnp.maximum(jnp.maximum(mine, col) - W, 0)
    hi = jnp.minimum(jnp.minimum(mine, col) + W, NG - 1)
    count = jnp.where(close(mine, col), jnp.maximum(hi - lo + 1, 0), 0)
    span = jnp.stack([jnp.minimum(lo, NG - 1), count, mine, col]).astype(jnp.int32)
    return multiply(span, slab_cols, window_cols, g, b)


def solution(mesh):
    in_specs = (P("rep", "row", "col"), P("rep", "row", "col"), P(), P())
    out_specs = P(("row", "rep"), "col")
    return jax.shard_map(body, mesh=mesh, in_specs=in_specs, out_specs=out_specs, check_vma=False)
```

time: 355 us -> 132 us (0.37)
  waiting for transfers between devices: 299 us -> 0 us
  Pallas kernels: 0 us -> 128 us
  matrix products: 31 us -> 0 us
  between operations: 13.2 us -> 0.01 us
  other arithmetic: 8.21 us -> 0.62 us
    all_gather x2 -> x0, waiting for transfers between devices: 263 us -> none  [the longest x1 212 us: body(): slab_whole = lax.all_gather(slab_kept, 'col', axis=1, tiled=True)]
    pallas_call x0 -> x2, Pallas kernels: none -> 128 us  [the longest x1 111 us: gather(): pl.pallas_call(gather_kernel, out_shape=(jax.ShapeDtypeStruct((G, KL, BS,...]
    reduce_scatter x1 -> x0, waiting for transfers between devices: 35.4 us -> none  [body(): lax.psum_scatter(partial_sum, 'rep', scatter_dimension=0, tiled=True)]
    dot_general x1 -> x0, matrix products: 31 us -> none  [product(): jnp.dot(left, right, precision=lax.Precision.HIGHEST, preferred_element_t...]
    mul x3 -> x0, other arithmetic: 5.99 us -> none  [the longest x1 2.49 us: body(): window_kept = window_local * expand(mine_b, BS)]
  transfers between devices with their start and end apart: 3 -> 0, of which waited for: 3 -> 0; matrix products, arithmetic and copies ran while one was open for 1% -> 0% of each run, Pallas kernels for 0% -> 0%
where the time goes in v2:
time: 132 us
  Pallas kernels  128 us (97%)
  local copies, waits for them, and re-layouts  2.82 us (2%)
    pallas_call x1, Pallas kernels, gather(): pl.pallas_call(gather_kernel, out_shape=(jax.ShapeDtypeStruct((G, KL, BS,...  111 us
    pallas_call x1, Pallas kernels, multiply(): pl.pallas_call(product_kernel, grid_spec=pltpu.PrefetchScalarGridSpec(num...  17.6 us
    unnamed x2, local copies, waits for them, and re-layouts  2.82 us

profile of v2, /device:TPU:10, one launch (start us, length us, event | category | flops | bytes accessed | tf_op | source)
XLA Modules:
  0.0 131.7 jit_solution(10639534533240522049)
XLA Ops:
  0.0 0.6 pad_add_fusion.span
  0.6 1.4 %copy.6.slab_cols = s32[64,20]{1,0:T(8,128)} copy(s32[64,20]{0,1:T(8,128)} %param.6) | data formatting | bytes 10240 | tf_op args[2]
  2.0 1.4 %copy.7.window_cols = s32[64,20]{1,0:T(8,128)} copy(s32[64,20]{0,1:T(8,128)} %param.7) | data formatting | bytes 10240 | tf_op args[3]
  3.4 110.7 %gather.1 = (f32[4,20,128,128]{3,2,1,0:T(8,128)}, f32[16,512,512]{2,1,0:T(8,128)}) custom-call(f32[1,1024,256]{2,1,0:T(8,128)} %slab.1, f32[1,512,512]{2,1,0:T(8,128)} %window.1, s32[64,20]{1,0:T(8,128)} %copy.6.slab_cols), custom_call_target="tpu_custom_call" | custom-call | tf_op jit(solution)/shard_map/gather/pallas_call | solution.py:259
  114.1 17.6 %multiply.1 = f32[512,512]{1,0:T(8,128)} custom-call(s32[4]{0:T(128)} %pad_add_fusion.span, s32[64,20]{1,0:T(8,128)} %copy.6.slab_cols, s32[64,20]{1,0:T(8,128)} %copy.7.window_cols, f32[4,20,128,128]{3,2,1,0:T(8,128)} %get-tuple-element.7.g_ref, f32[16,512,512]{2,1,0:T(8,128)} %get-tuple-element.8.b_ref), custom_call_target="tpu_custom_call" | custom-call | tf_op jit(solution)/shard_map/multiply/pallas_call | solution.py:331

commit v3 on v2

--- a/solution.py
+++ b/solution.py
@@ -23,8 +23,22 @@
     return (a - b <= W) & (b - a <= W)
 
 
-def gather_kernel(slab, window, slab_cols, g_out, b_out, strips, packed, bounce, local_sem, e_recv, g_recv, b_recv,
-                  share_recv, e_send, z_send, zr_send, y_send, yr_send, x_send, xr_send, c_send, s_send):
+def split(v):
+    high = v.astype(jnp.bfloat16)
+    return high, (v - high.astype(jnp.float32)).astype(jnp.bfloat16)
+
+
+def listed(table, at, first):
+    lane = lax.broadcasted_iota(jnp.int32, (1, T), 1) // BS
+    hit = jnp.zeros((1, T), jnp.float32)
+    for t in range(KL):
+        hit = jnp.where(lane == table[t, at] - first, 1.0, hit)
+    return hit
+
+
+def square_kernel(slab, window, slab_cols, window_cols, out, strips, blocks, tiles, high, low, local_sem, e_recv,
+                  g_recv, b_recv, share_recv, e_send, z_send, zr_send, y_send, yr_send, x_send, xr_send, c_send,
+                  s_send):
     row, col, rep = lax.axis_index("row"), lax.axis_index("col"), lax.axis_index("rep")
     x, core = row // 2, row % 2
     y, zh = col // NH, col % NH
@@ -92,7 +106,7 @@
     keep_strip.start()
 
     def b_half(k, h):
-        return b_out.at[k, pl.ds(h * HT, HT)]
+        return tiles.at[k, pl.ds(h * HT, HT)]
 
     def own_b(h):
         return window.at[0, pl.ds(h * HT, HT)]
@@ -126,8 +140,8 @@
     for h in range(2):
         begin(kb_in, send(own_b(h), b_half(kb, h), c_send.at[h], b_recv.at[kb, h], across))
     b_first(kb, own_b, 0)
-    take_b = pltpu.make_async_copy(window.at[0], bounce, local_sem.at[1])
-    take_b.start()
+    keep_tile = pltpu.make_async_copy(window.at[0], tiles.at[kb], local_sem.at[1])
+    keep_tile.start()
 
     def b_from(n, off):
         p = rep if n == 0 else 1 - rep
@@ -151,9 +165,6 @@
             landed(wants_b(k, x), b_half(k, h), b_recv.at[k, h])
             b_share(k, h, b_half(k, h), 2 + n * 3 + 2)
 
-    take_b.wait()
-    put_b = pltpu.make_async_copy(bounce, b_out.at[kb], local_sem.at[2])
-    put_b.start()
     b_relay(0)
 
     keep_strip.wait()
@@ -165,15 +176,15 @@
             q = (t % 2) * NG + ((y + oy) % NY) * NH + t // 2
             landed(close(mine, q // 2), strips.at[q], e_recv.at[q])
     for t in range(KL):
-        k = slab_cols[mine * G + y, t]
+        k = slab_cols[t, mine * G + y]
         both = strips[k // 2]
-        packed[t] = jnp.where(k % 2 == 0, both[:, :BS], both[:, BS:])
+        blocks[y, t, pl.ds(zh * ST, ST), :] = jnp.where(k % 2 == 0, both[:, :BS], both[:, BS:])
 
     def place(i, s, h):
-        return g_out.at[i, pl.ds(h * HK, HK), pl.ds(s * ST, ST)]
+        return blocks.at[i, pl.ds(h * HK, HK), pl.ds(s * ST, ST)]
 
     def own_g(h):
-        return packed.at[pl.ds(h * HK, HK)]
+        return place(y, zh, h)
 
     def g_send(src, i, s, h, sem, dest):
         return send(src, place(i, s, h), sem, g_recv.at[i, s, h], dest)
@@ -194,10 +205,10 @@
         for lead in range(2):
             h = lead
             begin(up | far if lead == 0 else up,
-                  g_send(own_g(h) if n == 0 else place(y, s, h), y, s, h, y_send.at[n, 0, h], at_y(1)))
+                  g_send(place(y, s, h), y, s, h, y_send.at[n, 0, h], at_y(1)))
             h = 1 - lead
             begin(down | far if lead == 0 else down,
-                  g_send(own_g(h) if n == 0 else place(y, s, h), y, s, h, y_send.at[n, 1, h], at_y(-1)))
+                  g_send(place(y, s, h), y, s, h, y_send.at[n, 1, h], at_y(-1)))
 
     def y_relay(n, off):
         s = (zh + off + NH) % NH
@@ -214,8 +225,6 @@
             landed(here, place(i, s, h), g_recv.at[i, s, h])
 
     y_first(0, 0)
-    put_g = pltpu.make_async_copy(packed, g_out.at[y, :, pl.ds(zh * ST, ST)], local_sem.at[3])
-    put_g.start()
 
     for h in range(2):
         landed(kc_in, b_half(kc, h), b_recv.at[kc, h])
@@ -241,115 +250,83 @@
     y_relay(3, 2)
     b_rest(1)
 
-    for n, off in enumerate((0, -1, 1, 2)):
-        y_rest(n, off)
     for m in range(8):
         k = m * 2 + 1 - core
         for h in range(2):
             landed(close(k, col) & close(mine, col) & close(mine, k), b_half(k, h), share_recv.at[k, h])
-    put_g.wait()
-    put_b.wait()
+    keep_tile.wait()
+
+    active = close(mine, col)
+    lo = jnp.maximum(jnp.maximum(mine, col) - W, 0)
+    hi = jnp.minimum(jnp.minimum(mine, col) + W, NG - 1)
+
+    @pl.when(active)
+    def _():
+        @pl.loop(lo, hi + 1)
+        def _(k):
+            for i in range(G):
+                keep = listed(window_cols, k * G + i, col * G)
+                h, l = split(tiles[k, i * BS:(i + 1) * BS] * keep)
+                high[k * G + i] = h
+                low[k * G + i] = l
+
+    for n, off in enumerate((0, -1, 1, 2)):
+        y_rest(n, off)
+
+    @pl.when(active)
+    def _():
+        @pl.loop(0, G)
+        def _(r):
+            at = mine * G + r
+            total = jnp.zeros((BS, T), jnp.float32)
+            for t in range(0, KL, 2):
+                a, bh, bl = [], [], []
+                for u in (t, t + 1):
+                    k = slab_cols[u, at]
+                    valid = (k >= lo * G) & (k < hi * G + G)
+                    k = jnp.where(valid, k, lo * G)
+                    a.append(blocks[r, u] * jnp.where(valid, 1.0, 0.0))
+                    bh.append(high[k])
+                    bl.append(low[k])
+                ah, al = split(jnp.concatenate(a, axis=1))
+                rh, rl = jnp.concatenate(bh, axis=0), jnp.concatenate(bl, axis=0)
+                two = jnp.dot(jnp.concatenate([ah, al], axis=0), rh, preferred_element_type=jnp.float32)
+                total = total + (two[:BS] + (two[BS:] + jnp.dot(ah, rl, preferred_element_type=jnp.float32)))
+            out[pl.ds(pl.multiple_of(r * BS, BS), BS), :] = total * listed(slab_cols, at, col * G)
+
+    @pl.when(jnp.logical_not(active))
+    def _():
+        out[...] = jnp.zeros_like(out)
+
     for end in later:
         end()
 
 
-def gather(slab, window, slab_cols):
+def square(slab, window, slab_cols, window_cols):
     dma = pltpu.SemaphoreType.DMA
     hbm = pl.BlockSpec(memory_space=pl.ANY)
+    table = pl.BlockSpec(memory_space=pltpu.SMEM)
     return pl.pallas_call(
-        gather_kernel,
-        out_shape=(jax.ShapeDtypeStruct((G, KL, BS, BS), jnp.float32),
-                   jax.ShapeDtypeStruct((NG, T, T), jnp.float32)),
-        in_specs=[hbm, hbm, pl.BlockSpec(memory_space=pltpu.SMEM)],
-        out_specs=(hbm, hbm),
+        square_kernel,
+        out_shape=jax.ShapeDtypeStruct((T, T), jnp.float32),
+        in_specs=[hbm, hbm, table, table],
+        out_specs=pl.BlockSpec(memory_space=pltpu.VMEM),
         scratch_shapes=[
-            pltpu.VMEM((2 * NG, ST, 2 * BS), jnp.float32), pltpu.VMEM((KL, ST, BS), jnp.float32),
-            pltpu.VMEM((T, T), jnp.float32),
-            dma((4,)), dma((2 * NG,)), dma((NY, NH, 2)), dma((NG, 2)), dma((NG, 2)),
+            pltpu.VMEM((2 * NG, ST, 2 * BS), jnp.float32), pltpu.VMEM((G, KL, BS, BS), jnp.float32),
+            pltpu.VMEM((NG, T, T), jnp.float32),
+            pltpu.VMEM((NG * G, BS, T), jnp.bfloat16), pltpu.VMEM((NG * G, BS, T), jnp.bfloat16),
+            dma((2,)), dma((2 * NG,)), dma((NY, NH, 2)), dma((NG, 2)), dma((NG, 2)),
             dma((31,)), dma((2, 2)), dma((2,)), dma((4, 2, 2)), dma((4, 2)),
             dma((2, 2, 2)), dma((2, 2)), dma((2,)), dma((8, 2)),
         ],
-        compiler_params=pltpu.CompilerParams(collective_id=0, has_side_effects=True),
-        name="gather",
-    )(slab, window, slab_cols)
-
-
-def split(v):
-    high = v.astype(jnp.bfloat16)
-    return high, (v - high.astype(jnp.float32)).astype(jnp.bfloat16)
-
-
-STEPS = 2 * W + 1
-
-
-def product_kernel(span, slab_cols, window_cols, g_ref, b_ref, out_ref, b_high, b_low):
-    s = pl.program_id(0)
-    lo, count, rows, cols = span[0], span[1], span[2], span[3]
-    lane = lax.broadcasted_iota(jnp.int32, (1, T), 1) // BS
-
-    def listed(table, at, first):
-        hit = jnp.zeros((1, T), jnp.float32)
-        for t in range(KL):
-            hit = jnp.where(lane == table[at, t] - first, 1.0, hit)
-        return hit
-
-    @pl.when(s < count)
-    def _():
-        for i in range(G):
-            keep = listed(window_cols, (lo + s) * G + i, cols * G)
-            high, low = split(b_ref[0, i * BS:(i + 1) * BS] * keep)
-            b_high[s * G + i] = high
-            b_low[s * G + i] = low
-
-    @pl.when((s >= STEPS) & (count == 0))
-    def _():
-        out_ref[...] = jnp.zeros_like(out_ref)
-
-    @pl.when((s >= STEPS) & (count > 0))
-    def _():
-        at = rows * G + s - STEPS
-        total = jnp.zeros((BS, T), jnp.float32)
-        for t in range(0, KL, 2):
-            left, high, low = [], [], []
-            for u in (t, t + 1):
-                k = slab_cols[at, u] - lo * G
-                valid = (k >= 0) & (k < count * G)
-                k = jnp.where(valid, k, 0)
-                left.append(g_ref[0, u] * jnp.where(valid, 1.0, 0.0))
-                high.append(b_high[k])
-                low.append(b_low[k])
-            lh, ll = split(jnp.concatenate(left, axis=1))
-            rh, rl = jnp.concatenate(high, axis=0), jnp.concatenate(low, axis=0)
-            two = jnp.dot(jnp.concatenate([lh, ll], axis=0), rh, preferred_element_type=jnp.float32)
-            total = total + (two[:BS] + (two[BS:] + jnp.dot(lh, rl, preferred_element_type=jnp.float32)))
-        out_ref[...] = total * listed(slab_cols, at, cols * G)
-
-
-def multiply(span, slab_cols, window_cols, g, b):
-    at_b = lambda s, span, *_: (span[0] + jnp.minimum(s, jnp.maximum(span[1] - 1, 0)), 0, 0)
-    at_g = lambda s, *_: (jnp.maximum(s - STEPS, 0), 0, 0, 0)
-    return pl.pallas_call(
-        product_kernel,
-        grid_spec=pltpu.PrefetchScalarGridSpec(
-            num_scalar_prefetch=3, grid=(STEPS + G,),
-            in_specs=[pl.BlockSpec((1, KL, BS, BS), at_g), pl.BlockSpec((1, T, T), at_b)],
-            out_specs=pl.BlockSpec((BS, T), lambda s, *_: (jnp.maximum(s - STEPS, 0), 0)),
-            scratch_shapes=[pltpu.VMEM((STEPS * G, BS, T), jnp.bfloat16)] * 2),
-        out_shape=jax.ShapeDtypeStruct((T, T), jnp.float32),
-        compiler_params=pltpu.CompilerParams(dimension_semantics=("arbitrary",)),
-        name="multiply",
-    )(span, slab_cols, window_cols, g, b)
+        compiler_params=pltpu.CompilerParams(
+            collective_id=0, has_side_effects=True, vmem_limit_bytes=60 << 20),
+        name="square",
+    )(slab, window, slab_cols, window_cols)
 
 
 def body(slab_half, window_half, slab_cols, window_cols):
-    mine = 2 * lax.axis_index("row") + lax.axis_index("rep")
-    col = lax.axis_index("col")
-    g, b = gather(slab_half, window_half, slab_cols)
-    lo = jnp.maximum(jnp.maximum(mine, col) - W, 0)
-    hi = jnp.minimum(jnp.minimum(mine, col) + W, NG - 1)
-    count = jnp.where(close(mine, col), jnp.maximum(hi - lo + 1, 0), 0)
-    span = jnp.stack([jnp.minimum(lo, NG - 1), count, mine, col]).astype(jnp.int32)
-    return multiply(span, slab_cols, window_cols, g, b)
+    return square(slab_half, window_half, slab_cols.T, window_cols.T)
 
 
 def solution(mesh):

time: 132 us -> 118 us (0.89)
  Pallas kernels: 128 us -> 116 us
    pallas_call x2 -> x1, Pallas kernels: 128 us -> 116 us  [square(): pl.pallas_call(square_kernel, out_shape=jax.ShapeDtypeStruct((T, T), jnp....]
    unnamed x2 -> x1, local copies, waits for them, and re-layouts: 2.82 us -> 2.26 us
where the time goes in v3:
time: 118 us
  Pallas kernels  116 us (98%)
  local copies, waits for them, and re-layouts  2.26 us (2%)
    pallas_call x1, Pallas kernels, square(): pl.pallas_call(square_kernel, out_shape=jax.ShapeDtypeStruct((T, T), jnp....  116 us

profile of v3, /device:TPU:10, one launch (start us, length us, event | category | flops | bytes accessed | tf_op | source)
XLA Modules:
  0.0 118.0 jit_solution(813024400025214547)
XLA Ops:
  0.0 115.8 %square.1 = f32[512,512]{1,0:T(8,128)} custom-call(f32[1,1024,256]{2,1,0:T(8,128)} %slab.1, f32[1,512,512]{2,1,0:T(8,128)} %window.1, s32[20,64]{1,0:T(8,128)} %bitcast.2, s32[20,64]{1,0:T(8,128)} %bitcast.3), custom_call_target="tpu_custom_call" | custom-call | tf_op jit(solution)/shard_map/square/pallas_call | solution.py:309
  115.8 2.3 %copy.6 = f32[512,512]{1,0:T(8,128)} copy(f32[512,512]{1,0:T(8,128)} %square.1) | data formatting | bytes 2097152

commit v4 on v3

v4 whole, which is shorter than its diff:
```python
import functools

import jax
import jax.numpy as jnp
from jax import lax
from jax.experimental import pallas as pl
from jax.experimental.pallas import tpu as pltpu
from jax.sharding import PartitionSpec as P

BS = 128
BAND = 24
KL = 20
MESH = pl.DeviceIdType.MESH
G = 4
W = BAND // G
NG = 16
T = G * BS
NX, NY, NZ, NH = 4, 4, 8, 4
ST = T // NG
CUT = (0, 10, KL)
HT = T // 2
ORDER = ("e", "f", "c0", "x", "b000", "b011", "p", "z", "c1", "y00", "y01", "k0", "zp0", "zp1", "b001", "b010", "zl0", "y10", "y11", "zl1", "y20", "y21", "k1", "r0", "bf0", "zf0", "zf1", "y30", "y31", "r1", "b100", "b111", "r2", "r3", "b101", "b110", "bf1")


def close(a, b):
    return (a - b <= W) & (b - a <= W)


def split(v):
    high = v.astype(jnp.bfloat16)
    return high, (v - high.astype(jnp.float32)).astype(jnp.bfloat16)


def listed(table, at, first):
    lane = lax.broadcasted_iota(jnp.int32, (1, T), 1) // BS
    hit = jnp.zeros((1, T), jnp.float32)
    for t in range(KL):
        hit = jnp.where(lane == table[t, at] - first, 1.0, hit)
    return hit


def square_kernel(slab, window, slab_cols, window_cols, out, strips, blocks, tiles, high, low, ready, local_sem, e_recv,
                  g_recv, b_recv, share_recv, e_send, z_send, zr_send, y_send, yr_send, x_send, xr_send, c_send,
                  s_send):
    row, col, rep = lax.axis_index("row"), lax.axis_index("col"), lax.axis_index("rep")
    x, core = row // 2, row % 2
    y, zh = col // NH, col % NH
    z = zh * 2 + rep
    mine = 2 * row + rep
    other = 2 * row + 1 - rep

    def at_plane(oy, oz):
        t = (z + oz) % NZ
        return {"row": row, "col": ((y + oy) % NY) * NH + t // 2, "rep": t % 2}

    def at_h(off):
        return {"row": row, "col": y * NH + (zh + off + NH) % NH, "rep": rep}

    def at_y(off):
        return {"row": row, "col": ((y + off + NY) % NY) * NH + zh, "rep": rep}

    def at_x(off):
        return {"row": ((x + off + NX) % NX) * 2 + core, "col": col, "rep": rep}

    partner = {"row": x * 2 + 1 - core, "col": col, "rep": rep}
    across = {"row": row, "col": col, "rep": 1 - rep}
    plane = [(oy, oz) for oz in (4, 3, 5, 2, 6, 1, 7, 0) for oy in (2, 1, 3, 0) if (oy, oz) != (0, 0)]

    barrier = pltpu.get_barrier_semaphore()
    near = [(oy, oz) for oy, oz in plane if oy == 0 or oz == 0]
    friends = [at_plane(oy, oz) for oy, oz in near] + [at_x(1), at_x(-1), partner]
    for f in friends:
        pl.semaphore_signal(barrier, inc=1, device_id=f, device_id_type=MESH)
    pl.semaphore_wait(barrier, len(friends))
    for oy in range(1, NY):
        pl.semaphore_signal(ready, inc=1, device_id=at_y(oy), device_id_type=MESH)

    later = []

    def begin(cond, copy):
        @pl.when(cond)
        def _():
            copy.start()

        @later.append
        def _():
            @pl.when(cond)
            def _():
                copy.wait_send()

    def send(src, dst, sem, recv, dest):
        return pltpu.make_async_remote_copy(
            src_ref=src, dst_ref=dst, send_sem=sem, recv_sem=recv, device_id=dest, device_id_type=MESH)

    def landed(cond, dst, recv):
        @pl.when(cond)
        def _():
            send(dst, dst, recv, recv, partner).wait_recv()

    q0 = rep * NG + col
    k0 = q0 // 2
    own_in, opp_in = close(mine, k0), close(other, k0)

    def rows_for(p, c):
        return slab.at[0, pl.ds(p * T + c * ST, ST)]

    keep_strip = pltpu.make_async_copy(rows_for(rep, col), strips.at[q0], local_sem.at[0])

    def exchange(close_by):
        if not close_by:
            pl.semaphore_wait(ready, NY - 1)
        for n, (oy, oz) in enumerate(plane):
            if ((oy, oz) in near) != close_by:
                continue
            d = at_plane(oy, oz)
            begin(own_in if oz % 2 == 0 else opp_in,
                  send(rows_for(d["rep"], d["col"]), strips.at[q0], e_send.at[n], e_recv.at[q0], d))
        if close_by:
            keep_strip.start()

    def b_half(k, h):
        return tiles.at[k, pl.ds(h * HT, HT)]

    def own_b(h):
        return window.at[0, pl.ds(h * HT, HT)]

    def wants_b(k, xd):
        first = 4 * ((xd + NX) % NX) + rep
        second = first + 2
        return close(k, col) & ((close(first, col) & close(first, k)) | (close(second, col) & close(second, k)))

    twin = 2 * (x * 2 + 1 - core) + rep

    def b_share(k, h, src, n):
        cond = close(k, col) & close(twin, col) & close(twin, k)
        begin(cond, send(src, b_half(k, h), s_send.at[n, h], share_recv.at[k, h], partner))

    def b_first(k, src, n, h):
        up, down, far = wants_b(k, x + 1), wants_b(k, x - 1), wants_b(k, x + 2)
        far_up, far_down = far_ways(up, down, far, h)
        begin(up | far_up, send(src(h), b_half(k, h), x_send.at[n, 0, h], b_recv.at[k, h], at_x(1)))
        begin(down | far_down, send(src(h), b_half(k, h), x_send.at[n, 1, h], b_recv.at[k, h], at_x(-1)))

    nothing = rep < 0

    def far_ways(up, down, far, h):
        return (far, nothing) if h == 0 else (nothing, far)

    kb = rep * 8 + row
    kc = (1 - rep) * 8 + row
    kb_in, kc_in = close(kb, col), close(kc, col)
    keep_tile = pltpu.make_async_copy(window.at[0], tiles.at[kb], local_sem.at[1])

    def cross(h):
        begin(kb_in, send(own_b(h), b_half(kb, h), c_send.at[h], b_recv.at[kb, h], across))

    def own_tile():
        for h in range(2):
            b_first(kb, own_b, 0, h)
        for h in range(2):
            b_share(kb, h, own_b(h), 0)
        keep_tile.start()

    def crossed(h):
        landed(kc_in, b_half(kc, h), b_recv.at[kc, h])
        b_first(kc, lambda h: b_half(kc, h), 1, h)
        b_share(kc, h, b_half(kc, h), 1)

    def b_from(n, off):
        p = rep if n == 0 else 1 - rep
        return p * 8 + ((x + off + NX) % NX) * 2 + core

    def from_side(n, off, h):
        k = b_from(n, off)
        up, down, far = wants_b(k, x - off + 1), wants_b(k, x - off - 1), wants_b(k, x - off)
        k_up, k_down, k_far = wants_b(k, x + off + 1), wants_b(k, x + off - 1), wants_b(k, x + off + 2)
        far_up, far_down = far_ways(k_up, k_down, k_far, h)
        onward = far_up if off == -1 else far_down
        landed(wants_b(k, x) | onward, b_half(k, h), b_recv.at[k, h])
        begin(onward, send(b_half(k, h), b_half(k, h), xr_send.at[n, (off + 1) // 2, h], b_recv.at[k, h], at_x(-off)))
        b_share(k, h, b_half(k, h), 2 + n * 3 + (off + 1) // 2)

    def from_far(n):
        k = b_from(n, 2)
        for h in range(2):
            landed(wants_b(k, x), b_half(k, h), b_recv.at[k, h])
            b_share(k, h, b_half(k, h), 2 + n * 3 + 2)

    def pack():
        keep_strip.wait()
        for oz in range(NZ):
            for oy in range(NY):
                if (oy, oz) == (0, 0):
                    continue
                t = (z + oz) % NZ
                q = (t % 2) * NG + ((y + oy) % NY) * NH + t // 2
                landed(close(mine, q // 2), strips.at[q], e_recv.at[q])
        for t in range(KL):
            k = slab_cols[t, mine * G + y]
            both = strips[k // 2]
            blocks[y, t, pl.ds(zh * ST, ST), :] = jnp.where(k % 2 == 0, both[:, :BS], both[:, BS:])

    def place(i, s, h):
        return blocks.at[i, pl.ds(CUT[h], CUT[h + 1] - CUT[h]), pl.ds(s * ST, ST)]

    def g_send(i, s, h, sem, dest):
        return send(place(i, s, h), place(i, s, h), sem, g_recv.at[i, s, h], dest)

    always = rep >= 0

    def wants_g(yd):
        return close(mine, ((yd + NY) % NY) * NH + zh)

    here, up, down, far = wants_g(y), wants_g(y + 1), wants_g(y - 1), wants_g(y + 2)

    def z_own():
        for lead in range(2):
            begin(always, g_send(y, zh, lead, z_send.at[0, lead], at_h(1)))
            begin(always, g_send(y, zh, 1 - lead, z_send.at[1, 1 - lead], at_h(-1)))

    def z_pass(n, off, h):
        s = (zh + off + NH) % NH
        landed(always, place(y, s, h), g_recv.at[y, s, h])
        begin(always, g_send(y, s, h, zr_send.at[h], at_h(-off)))

    def z_land(off, h):
        s = (zh + off + NH) % NH
        landed(always, place(y, s, h), g_recv.at[y, s, h])

    def y_first(n, off, h):
        s = (zh + off + NH) % NH
        begin(up | far if h == 0 else up, g_send(y, s, h, y_send.at[n, 0, h], at_y(1)))
        begin(down | far if h == 1 else down, g_send(y, s, h, y_send.at[n, 1, h], at_y(-1)))

    def y_relay(n, off):
        s = (zh + off + NH) % NH
        for d, h in ((-1, 0), (1, 1)):
            i = (y + d + NY) % NY
            onward = wants_g(y - d)
            landed(here | onward, place(i, s, h), g_recv.at[i, s, h])
            begin(onward, g_send(i, s, h, yr_send.at[n, h], at_y(-d)))

    def row_rest(d):
        i = (y + d + NY) % NY
        for off in OFFS:
            t = (zh + off + NH) % NH
            for h in ((), (1,), (0,), (0, 1))[(0, -1, 1, 2).index(d)]:
                landed(here, place(i, t, h), g_recv.at[i, t, h])

    OFFS = (0, -1, 1, 2)
    steps = {"e": functools.partial(exchange, True), "f": functools.partial(exchange, False), "x": own_tile, "p": pack, "z": z_own}
    for h in range(2):
        steps["c%d" % h] = functools.partial(cross, h)
        steps["k%d" % h] = functools.partial(crossed, h)
        steps["zp%d" % h] = functools.partial(z_pass, 1 + h, 2 * h - 1, h)
        steps["zl%d" % h] = functools.partial(z_land, 2 * h - 1, 1 - h)
        steps["zf%d" % h] = functools.partial(z_land, 2, h)
        steps["bf%d" % h] = functools.partial(from_far, h)
        for n in range(4):
            steps["y%d%d" % (n, h)] = functools.partial(y_first, n, OFFS[n], h)
        for n in range(2):
            for w in range(2):
                steps["b%d%d%d" % (n, w, h)] = functools.partial(from_side, n, 2 * w - 1, h)
    for n in range(4):
        steps["r%d" % n] = functools.partial(y_relay, n, OFFS[n])
    for step in ORDER:
        steps[step]()

    for m in range(8):
        k = m * 2 + 1 - core
        for h in range(2):
            landed(close(k, col) & close(mine, col) & close(mine, k), b_half(k, h), share_recv.at[k, h])
    keep_tile.wait()

    active = close(mine, col)
    lo = jnp.maximum(jnp.maximum(mine, col) - W, 0)
    hi = jnp.minimum(jnp.minimum(mine, col) + W, NG - 1)

    @pl.when(active)
    def _():
        @pl.loop(lo, hi + 1)
        def _(k):
            for i in range(G):
                keep = listed(window_cols, k * G + i, col * G)
                h, l = split(tiles[k, i * BS:(i + 1) * BS] * keep)
                high[k * G + i] = h
                low[k * G + i] = l

    def multiply(r):
        at = mine * G + r
        total = jnp.zeros((BS, T), jnp.float32)
        for t in range(0, KL, 2):
            a, bh, bl = [], [], []
            for u in (t, t + 1):
                k = slab_cols[u, at]
                valid = (k >= lo * G) & (k < hi * G + G)
                k = jnp.where(valid, k, lo * G)
                a.append(blocks[r, u] * jnp.where(valid, 1.0, 0.0))
                bh.append(high[k])
                bl.append(low[k])
            ah, al = split(jnp.concatenate(a, axis=1))
            rh, rl = jnp.concatenate(bh, axis=0), jnp.concatenate(bl, axis=0)
            two = jnp.dot(jnp.concatenate([ah, al], axis=0), rh, preferred_element_type=jnp.float32)
            total = total + (two[:BS] + (two[BS:] + jnp.dot(ah, rl, preferred_element_type=jnp.float32)))
        out[pl.ds(pl.multiple_of(r * BS, BS), BS), :] = total * listed(slab_cols, at, col * G)

    for d in (0, -1, 1, 2):
        row_rest(d)

        @pl.when(active)
        def _():
            multiply((y + d + NY) % NY)

    @pl.when(jnp.logical_not(active))
    def _():
        out[...] = jnp.zeros_like(out)

    for end in later:
        end()


def square(slab, window, slab_cols, window_cols):
    dma = pltpu.SemaphoreType.DMA
    hbm = pl.BlockSpec(memory_space=pl.ANY)
    table = pl.BlockSpec(memory_space=pltpu.SMEM)
    return pl.pallas_call(
        square_kernel,
        out_shape=jax.ShapeDtypeStruct((T, T), jnp.float32),
        in_specs=[hbm, hbm, table, table],
        out_specs=pl.BlockSpec(memory_space=pltpu.VMEM),
        scratch_shapes=[
            pltpu.VMEM((2 * NG, ST, 2 * BS), jnp.float32), pltpu.VMEM((G, KL, BS, BS), jnp.float32),
            pltpu.VMEM((NG, T, T), jnp.float32),
            pltpu.VMEM((NG * G, BS, T), jnp.bfloat16), pltpu.VMEM((NG * G, BS, T), jnp.bfloat16),
            pltpu.SemaphoreType.REGULAR, dma((2,)), dma((2 * NG,)), dma((NY, NH, 2)), dma((NG, 2)), dma((NG, 2)),
            dma((31,)), dma((2, 2)), dma((2,)), dma((4, 2, 2)), dma((4, 2)),
            dma((2, 2, 2)), dma((2, 2, 2)), dma((2,)), dma((8, 2)),
        ],
        compiler_params=pltpu.CompilerParams(
            collective_id=0, has_side_effects=True, vmem_limit_bytes=60 << 20),
        name="square",
    )(slab, window, slab_cols, window_cols)


def body(slab_half, window_half, slab_cols, window_cols):
    return square(slab_half, window_half, slab_cols.T, window_cols.T)


def solution(mesh):
    in_specs = (P("rep", "row", "col"), P("rep", "row", "col"), P(), P())
    out_specs = P(("row", "rep"), "col")
    return jax.shard_map(body, mesh=mesh, in_specs=in_specs, out_specs=out_specs, check_vma=False)
```

time: 118 us -> 112 us (0.949)
  the two profiles are of different devices: /device:TPU:10 before, /device:TPU:31 now
where the time goes in v4:
time: 112 us; the launch traced here: 111 us
  Pallas kernels  109 us (97%)
  local copies, waits for them, and re-layouts  2.26 us (2%)
    pallas_call x1, Pallas kernels, square(): pl.pallas_call(square_kernel, out_shape=jax.ShapeDtypeStruct((T, T), jnp....  109 us
    unnamed x1, local copies, waits for them, and re-layouts  2.26 us

profile of v4, /device:TPU:31, one launch (start us, length us, event | category | flops | bytes accessed | tf_op | source)
XLA Modules:
  0.0 111.4 jit_solution(11015447909675289730)
XLA Ops:
  0.0 109.1 %square.1 = f32[512,512]{1,0:T(8,128)} custom-call(f32[1,1024,256]{2,1,0:T(8,128)} %slab.1, f32[1,512,512]{2,1,0:T(8,128)} %window.1, s32[20,64]{1,0:T(8,128)} %bitcast.2, s32[20,64]{1,0:T(8,128)} %bitcast.3), custom_call_target="tpu_custom_call" | custom-call | tf_op jit(solution)/shard_map/square/pallas_call | solution.py:326
  109.1 2.3 %copy.6 = f32[512,512]{1,0:T(8,128)} copy(f32[512,512]{1,0:T(8,128)} %square.1) | data formatting | bytes 2097152

commit v5 on v4

--- a/solution.py
+++ b/solution.py
@@ -17,9 +17,9 @@
 T = G * BS
 NX, NY, NZ, NH = 4, 4, 8, 4
 ST = T // NG
-CUT = (0, 10, KL)
+SH = ST // 2
 HT = T // 2
-ORDER = ("e", "f", "c0", "x", "b000", "b011", "p", "z", "c1", "y00", "y01", "k0", "zp0", "zp1", "b001", "b010", "zl0", "y10", "y11", "zl1", "y20", "y21", "k1", "r0", "bf0", "zf0", "zf1", "y30", "y31", "r1", "b100", "b111", "r2", "r3", "b101", "b110", "bf1")
+ORDER = ("e0", "f0", "c0", "x", "e1", "f1", "b000", "b011", "p0", "z0", "y00", "c1", "p1", "z1", "y01", "k0", "zp0", "y10", "zl1", "y20", "k1", "b001", "b010", "zp1", "y21", "zl0", "y11", "r00", "r01", "zf0", "y30", "zf1", "y31", "b100", "b111", "r10", "r11", "bf0", "r20", "r21", "r30", "r31", "b101", "b110", "bf1")
 
 
 def close(a, b):
@@ -39,7 +39,7 @@
     return hit
 
 
-def square_kernel(slab, window, slab_cols, window_cols, out, strips, blocks, tiles, high, low, ready, local_sem, e_recv,
+def square_kernel(slab, window, slab_cols, window_cols, out, strips_0, strips_1, blocks, tiles, high, low, ready, local_sem, e_recv,
                   g_recv, b_recv, share_recv, e_send, z_send, zr_send, y_send, yr_send, x_send, xr_send, c_send,
                   s_send):
     row, col, rep = lax.axis_index("row"), lax.axis_index("col"), lax.axis_index("rep")
@@ -101,22 +101,27 @@
     k0 = q0 // 2
     own_in, opp_in = close(mine, k0), close(other, k0)
 
-    def rows_for(p, c):
-        return slab.at[0, pl.ds(p * T + c * ST, ST)]
-
-    keep_strip = pltpu.make_async_copy(rows_for(rep, col), strips.at[q0], local_sem.at[0])
-
-    def exchange(close_by):
-        if not close_by:
+    def rows_for(p, c, h):
+        return slab.at[0, pl.ds(p * T + c * ST + h * SH, SH)]
+
+    strips = (strips_0, strips_1)
+
+    def strip(q, h):
+        return strips[h].at[q]
+
+    keep_strip = [pltpu.make_async_copy(rows_for(rep, col, h), strip(q0, h), local_sem.at[h]) for h in range(2)]
+
+    def exchange(close_by, h):
+        if not close_by and h == 0:
             pl.semaphore_wait(ready, NY - 1)
         for n, (oy, oz) in enumerate(plane):
             if ((oy, oz) in near) != close_by:
                 continue
             d = at_plane(oy, oz)
             begin(own_in if oz % 2 == 0 else opp_in,
-                  send(rows_for(d["rep"], d["col"]), strips.at[q0], e_send.at[n], e_recv.at[q0], d))
+                  send(rows_for(d["rep"], d["col"], h), strip(q0, h), e_send.at[n, h], e_recv.at[q0, h], d))
         if close_by:
-            keep_strip.start()
+            keep_strip[h].start()
 
     def b_half(k, h):
         return tiles.at[k, pl.ds(h * HT, HT)]
@@ -149,7 +154,7 @@
     kb = rep * 8 + row
     kc = (1 - rep) * 8 + row
     kb_in, kc_in = close(kb, col), close(kc, col)
-    keep_tile = pltpu.make_async_copy(window.at[0], tiles.at[kb], local_sem.at[1])
+    keep_tile = pltpu.make_async_copy(window.at[0], tiles.at[kb], local_sem.at[2])
 
     def cross(h):
         begin(kb_in, send(own_b(h), b_half(kb, h), c_send.at[h], b_recv.at[kb, h], across))
@@ -186,22 +191,22 @@
             landed(wants_b(k, x), b_half(k, h), b_recv.at[k, h])
             b_share(k, h, b_half(k, h), 2 + n * 3 + 2)
 
-    def pack():
-        keep_strip.wait()
+    def pack(h):
+        keep_strip[h].wait()
         for oz in range(NZ):
             for oy in range(NY):
                 if (oy, oz) == (0, 0):
                     continue
                 t = (z + oz) % NZ
                 q = (t % 2) * NG + ((y + oy) % NY) * NH + t // 2
-                landed(close(mine, q // 2), strips.at[q], e_recv.at[q])
+                landed(close(mine, q // 2), strip(q, h), e_recv.at[q, h])
         for t in range(KL):
             k = slab_cols[t, mine * G + y]
-            both = strips[k // 2]
-            blocks[y, t, pl.ds(zh * ST, ST), :] = jnp.where(k % 2 == 0, both[:, :BS], both[:, BS:])
+            both = strips[h][k // 2]
+            blocks[y, t, pl.ds(zh * ST + h * SH, SH), :] = jnp.where(k % 2 == 0, both[:, :BS], both[:, BS:])
 
     def place(i, s, h):
-        return blocks.at[i, pl.ds(CUT[h], CUT[h + 1] - CUT[h]), pl.ds(s * ST, ST)]
+        return blocks.at[i, :, pl.ds(s * ST + h * SH, SH)]
 
     def g_send(i, s, h, sem, dest):
         return send(place(i, s, h), place(i, s, h), sem, g_recv.at[i, s, h], dest)
@@ -213,10 +218,9 @@
 
     here, up, down, far = wants_g(y), wants_g(y + 1), wants_g(y - 1), wants_g(y + 2)
 
-    def z_own():
-        for lead in range(2):
-            begin(always, g_send(y, zh, lead, z_send.at[0, lead], at_h(1)))
-            begin(always, g_send(y, zh, 1 - lead, z_send.at[1, 1 - lead], at_h(-1)))
+    def z_own(h):
+        begin(always, g_send(y, zh, h, z_send.at[0, h], at_h(1)))
+        begin(always, g_send(y, zh, h, z_send.at[1, h], at_h(-1)))
 
     def z_pass(n, off, h):
         s = (zh + off + NH) % NH
@@ -232,13 +236,13 @@
         begin(up | far if h == 0 else up, g_send(y, s, h, y_send.at[n, 0, h], at_y(1)))
         begin(down | far if h == 1 else down, g_send(y, s, h, y_send.at[n, 1, h], at_y(-1)))
 
-    def y_relay(n, off):
+    def y_relay(n, off, h):
         s = (zh + off + NH) % NH
-        for d, h in ((-1, 0), (1, 1)):
-            i = (y + d + NY) % NY
-            onward = wants_g(y - d)
-            landed(here | onward, place(i, s, h), g_recv.at[i, s, h])
-            begin(onward, g_send(i, s, h, yr_send.at[n, h], at_y(-d)))
+        d = 2 * h - 1
+        i = (y + d + NY) % NY
+        onward = wants_g(y - d)
+        landed(here | onward, place(i, s, h), g_recv.at[i, s, h])
+        begin(onward, g_send(i, s, h, yr_send.at[n, h], at_y(-d)))
 
     def row_rest(d):
         i = (y + d + NY) % NY
@@ -248,8 +252,12 @@
                 landed(here, place(i, t, h), g_recv.at[i, t, h])
 
     OFFS = (0, -1, 1, 2)
-    steps = {"e": functools.partial(exchange, True), "f": functools.partial(exchange, False), "x": own_tile, "p": pack, "z": z_own}
+    steps = {"x": own_tile}
     for h in range(2):
+        steps["e%d" % h] = functools.partial(exchange, True, h)
+        steps["f%d" % h] = functools.partial(exchange, False, h)
+        steps["p%d" % h] = functools.partial(pack, h)
+        steps["z%d" % h] = functools.partial(z_own, h)
         steps["c%d" % h] = functools.partial(cross, h)
         steps["k%d" % h] = functools.partial(crossed, h)
         steps["zp%d" % h] = functools.partial(z_pass, 1 + h, 2 * h - 1, h)
@@ -258,11 +266,10 @@
         steps["bf%d" % h] = functools.partial(from_far, h)
         for n in range(4):
             steps["y%d%d" % (n, h)] = functools.partial(y_first, n, OFFS[n], h)
+            steps["r%d%d" % (n, h)] = functools.partial(y_relay, n, OFFS[n], h)
         for n in range(2):
             for w in range(2):
                 steps["b%d%d%d" % (n, w, h)] = functools.partial(from_side, n, 2 * w - 1, h)
-    for n in range(4):
-        steps["r%d" % n] = functools.partial(y_relay, n, OFFS[n])
     for step in ORDER:
         steps[step]()
 
@@ -329,11 +336,12 @@
         in_specs=[hbm, hbm, table, table],
         out_specs=pl.BlockSpec(memory_space=pltpu.VMEM),
         scratch_shapes=[
-            pltpu.VMEM((2 * NG, ST, 2 * BS), jnp.float32), pltpu.VMEM((G, KL, BS, BS), jnp.float32),
+            pltpu.VMEM((2 * NG, SH, 2 * BS), jnp.float32), pltpu.VMEM((2 * NG, SH, 2 * BS), jnp.float32),
+            pltpu.VMEM((G, KL, BS, BS), jnp.float32),
             pltpu.VMEM((NG, T, T), jnp.float32),
             pltpu.VMEM((NG * G, BS, T), jnp.bfloat16), pltpu.VMEM((NG * G, BS, T), jnp.bfloat16),
-            pltpu.SemaphoreType.REGULAR, dma((2,)), dma((2 * NG,)), dma((NY, NH, 2)), dma((NG, 2)), dma((NG, 2)),
-            dma((31,)), dma((2, 2)), dma((2,)), dma((4, 2, 2)), dma((4, 2)),
+            pltpu.SemaphoreType.REGULAR, dma((3,)), dma((2 * NG, 2)), dma((NY, NH, 2)), dma((NG, 2)), dma((NG, 2)),
+            dma((31, 2)), dma((2, 2)), dma((2,)), dma((4, 2, 2)), dma((4, 2)),
             dma((2, 2, 2)), dma((2, 2, 2)), dma((2,)), dma((8, 2)),
         ],
         compiler_params=pltpu.CompilerParams(

time: 112 us -> 108 us (0.964)
  the two profiles are of different devices: /device:TPU:31 before, /device:TPU:10 now
where the time goes in v5:
time: 108 us; the launch traced here: 107 us
  Pallas kernels  104 us (96%)
  local copies, waits for them, and re-layouts  2.26 us (2%)
    pallas_call x1, Pallas kernels, square(): pl.pallas_call(square_kernel, out_shape=jax.ShapeDtypeStruct((T, T), jnp....  104 us
    unnamed x1, local copies, waits for them, and re-layouts  2.26 us

profile of v5, /device:TPU:10, one launch (start us, length us, event | category | flops | bytes accessed | tf_op | source)
XLA Modules:
  0.0 106.5 jit_solution(17808177571734226687)
XLA Ops:
  0.0 104.3 %square.1 = f32[512,512]{1,0:T(8,128)} custom-call(f32[1,1024,256]{2,1,0:T(8,128)} %slab.1, f32[1,512,512]{2,1,0:T(8,128)} %window.1, s32[20,64]{1,0:T(8,128)} %bitcast.2, s32[20,64]{1,0:T(8,128)} %bitcast.3), custom_call_target="tpu_custom_call" | custom-call | tf_op jit(solution)/shard_map/square/pallas_call | solution.py:333
  104.3 2.3 %copy.6 = f32[512,512]{1,0:T(8,128)} copy(f32[512,512]{1,0:T(8,128)} %square.1) | data formatting | bytes 2097152

commit v6 on v5

--- a/solution.py
+++ b/solution.py
@@ -19,11 +19,15 @@
 ST = T // NG
 SH = ST // 2
 HT = T // 2
-ORDER = ("e0", "f0", "c0", "x", "e1", "f1", "b000", "b011", "p0", "z0", "y00", "c1", "p1", "z1", "y01", "k0", "zp0", "y10", "zl1", "y20", "k1", "b001", "b010", "zp1", "y21", "zl0", "y11", "r00", "r01", "zf0", "y30", "zf1", "y31", "b100", "b111", "r10", "r11", "bf0", "r20", "r21", "r30", "r31", "b101", "b110", "bf1")
+ORDER = ("c0", "e0", "f0", "x", "e1", "f1", "b000", "b011", "p0", "z0", "y00", "c1", "p1", "z1", "y01", "k0", "zp0", "y10", "zl1", "y20", "k1", "b001", "b010", "zp1", "y21", "zl0", "y11", "r00", "r01", "zf0", "y30", "zf1", "y31", "b100", "b111", "r10", "r11", "bf0", "r20", "r21", "r30", "r31", "b101", "b110", "bf1")
 
 
 def close(a, b):
     return (a - b <= W) & (b - a <= W)
+
+
+def within(i, q):
+    return (i - 2 * q - 1 <= BAND) & (2 * q - i <= BAND)
 
 
 def split(v):
@@ -98,8 +102,6 @@
             send(dst, dst, recv, recv, partner).wait_recv()
 
     q0 = rep * NG + col
-    k0 = q0 // 2
-    own_in, opp_in = close(mine, k0), close(other, k0)
 
     def rows_for(p, c, h):
         return slab.at[0, pl.ds(p * T + c * ST + h * SH, SH)]
@@ -118,7 +120,8 @@
             if ((oy, oz) in near) != close_by:
                 continue
             d = at_plane(oy, oz)
-            begin(own_in if oz % 2 == 0 else opp_in,
+            target = mine if oz % 2 == 0 else other
+            begin(within(target * G + (y + oy) % NY, q0),
                   send(rows_for(d["rep"], d["col"], h), strip(q0, h), e_send.at[n, h], e_recv.at[q0, h], d))
         if close_by:
             keep_strip[h].start()
@@ -199,7 +202,7 @@
                     continue
                 t = (z + oz) % NZ
                 q = (t % 2) * NG + ((y + oy) % NY) * NH + t // 2
-                landed(close(mine, q // 2), strip(q, h), e_recv.at[q, h])
+                landed(within(mine * G + y, q), strip(q, h), e_recv.at[q, h])
         for t in range(KL):
             k = slab_cols[t, mine * G + y]
             both = strips[h][k // 2]

time: 108 us -> 107 us (level)
  no operation moved by 1% of the time
where the time goes in v6:
time: 107 us; the launch traced here: 106 us
  Pallas kernels  103 us (96%)
  local copies, waits for them, and re-layouts  2.26 us (2%)
    pallas_call x1, Pallas kernels, square(): pl.pallas_call(square_kernel, out_shape=jax.ShapeDtypeStruct((T, T), jnp....  103 us
    unnamed x1, local copies, waits for them, and re-layouts  2.26 us

profile of v6, /device:TPU:10, one launch (start us, length us, event | category | flops | bytes accessed | tf_op | source)
XLA Modules:
  0.0 105.6 jit_solution(3774630555497933167)
XLA Ops:
  0.0 103.4 %square.1 = f32[512,512]{1,0:T(8,128)} custom-call(f32[1,1024,256]{2,1,0:T(8,128)} %slab.1, f32[1,512,512]{2,1,0:T(8,128)} %window.1, s32[20,64]{1,0:T(8,128)} %bitcast.2, s32[20,64]{1,0:T(8,128)} %bitcast.3), custom_call_target="tpu_custom_call" | custom-call | tf_op jit(solution)/shard_map/square/pallas_call | solution.py:336
  103.4 2.3 %copy.6 = f32[512,512]{1,0:T(8,128)} copy(f32[512,512]{1,0:T(8,128)} %square.1) | data formatting | bytes 2097152

commit v7 on v6

--- a/solution.py
+++ b/solution.py
@@ -143,11 +143,12 @@
         cond = close(k, col) & close(twin, col) & close(twin, k)
         begin(cond, send(src, b_half(k, h), s_send.at[n, h], share_recv.at[k, h], partner))
 
-    def b_first(k, src, n, h):
+    def b_first(k, src, n, h, ways=(0, 1)):
         up, down, far = wants_b(k, x + 1), wants_b(k, x - 1), wants_b(k, x + 2)
         far_up, far_down = far_ways(up, down, far, h)
-        begin(up | far_up, send(src(h), b_half(k, h), x_send.at[n, 0, h], b_recv.at[k, h], at_x(1)))
-        begin(down | far_down, send(src(h), b_half(k, h), x_send.at[n, 1, h], b_recv.at[k, h], at_x(-1)))
+        for w in ways:
+            begin((up | far_up, down | far_down)[w],
+                  send(src(h), b_half(k, h), x_send.at[n, w, h], b_recv.at[k, h], at_x(1 - 2 * w)))
 
     nothing = rep < 0
 
@@ -163,8 +164,9 @@
         begin(kb_in, send(own_b(h), b_half(kb, h), c_send.at[h], b_recv.at[kb, h], across))
 
     def own_tile():
-        for h in range(2):
-            b_first(kb, own_b, 0, h)
+        for lead in range(2):
+            b_first(kb, own_b, 0, lead, (0,))
+            b_first(kb, own_b, 0, 1 - lead, (1,))
         for h in range(2):
             b_share(kb, h, own_b(h), 0)
         keep_tile.start()

time: 107 us -> 107 us (level)
  no operation moved by 1% of the time
where the time goes in v7:
time: 107 us; the launch traced here: 106 us
  Pallas kernels  103 us (96%)
  local copies, waits for them, and re-layouts  2.26 us (2%)
    pallas_call x1, Pallas kernels, square(): pl.pallas_call(square_kernel, out_shape=jax.ShapeDtypeStruct((T, T), jnp....  103 us
    unnamed x1, local copies, waits for them, and re-layouts  2.26 us

profile of v7, /device:TPU:10, one launch (start us, length us, event | category | flops | bytes accessed | tf_op | source)
XLA Modules:
  0.0 105.6 jit_solution(2715787697467741486)
XLA Ops:
  0.0 103.4 %square.1 = f32[512,512]{1,0:T(8,128)} custom-call(f32[1,1024,256]{2,1,0:T(8,128)} %slab.1, f32[1,512,512]{2,1,0:T(8,128)} %window.1, s32[20,64]{1,0:T(8,128)} %bitcast.2, s32[20,64]{1,0:T(8,128)} %bitcast.3), custom_call_target="tpu_custom_call" | custom-call | tf_op jit(solution)/shard_map/square/pallas_call | solution.py:338
  103.4 2.3 %copy.6 = f32[512,512]{1,0:T(8,128)} copy(f32[512,512]{1,0:T(8,128)} %square.1) | data formatting | bytes 2097152
